TPU v7x, 32 devices: a whole 2x2x4 slice. The times are simulated.
32 devices in a mesh: row: 8 (over z, core), col: 4 (over y, x).
Axes of the slice: x: 2, y: 2, z: 4, core: 2. Of those that a mesh axis runs over, the one named last changes fastest.
Arguments:
- matrix: float32 [8192, 4096], P('row', 'col'), may hold values from -6 to 166
Outputs:
- updated: float32 [8192, 4096], P('row', 'col')
All inputs are finite; a program needn't handle non-finite values.
Results may differ from a plain program's by a relative error of at most 0.0003.
Values sent between devices are 32-bit elements; how exact they have to be, the bound alone decides.
No kernel may reach another device: no remote copies, remote signals or barrier semaphores. Data moves between devices by JAX's collectives and lax.ppermute only.
A program may use at most 64 MiB of HBM per device.

v0:
```python
import jax
import jax.numpy as jnp
from jax import lax
from jax.sharding import PartitionSpec as P

NB = 128


def from_root(value, axis, source):
    kept = jnp.where(lax.axis_index(axis) == source, value, 0).astype(value.dtype)
    return lax.psum(kept, axis)


def factor(corner):
    symmetric = jnp.tril(corner) + jnp.tril(corner, -1).T
    lower_factor = jnp.linalg.cholesky(symmetric)
    identity = jnp.eye(corner.shape[0], dtype=jnp.float32)
    inverse = jax.scipy.linalg.solve_triangular(lower_factor, identity, lower=True)
    return (lower_factor, inverse)


def body(matrix):
    rows_here = lax.axis_size("row")
    cols_here = lax.axis_size("col")
    row_index = lax.axis_index("row")
    col_index = lax.axis_index("col")
    row_blocks = matrix.shape[0] // NB
    col_blocks = matrix.shape[1] // NB
    corner = matrix[:NB, :NB]
    local_factor, local_inverse = factor(corner)
    stacked = from_root(jnp.stack([local_factor, local_inverse]), "row", 0)
    lower_factor = stacked[0]
    inverse = stacked[1]
    panel = lax.dot_general(
        matrix[:, :NB],
        inverse,
        (((1,), (1,)), ((), ())),
        precision=lax.Precision.HIGHEST,
        preferred_element_type=jnp.float32,
    )
    panel = panel.at[:NB].set(jnp.where(row_index == 0, lower_factor, panel[:NB]))
    panel = from_root(panel, "col", 0)
    whole = lax.all_gather(panel, "row", axis=0, tiled=True)
    all_blocks = whole.reshape(rows_here * row_blocks, NB, NB)
    wanted = jnp.arange(col_blocks, dtype=jnp.int32) * cols_here + col_index
    source_rows = wanted % rows_here * row_blocks + wanted // rows_here
    mirror = jnp.take(all_blocks, source_rows, axis=0).reshape(col_blocks * NB, NB)
    product = lax.dot_general(
        panel,
        mirror,
        (((1,), (1,)), ((), ())),
        precision=lax.Precision.HIGHEST,
        preferred_element_type=jnp.float32,
    )
    fresh = matrix - product
    global_rows = jnp.arange(row_blocks, dtype=jnp.int32) * rows_here + row_index
    global_cols = jnp.arange(col_blocks, dtype=jnp.int32) * cols_here + col_index
    keep_mask = (global_rows[:, None] >= global_cols[None, :]) & (global_cols[None, :] >= 1)
    shaped_old = matrix.reshape(row_blocks, NB, col_blocks, NB)
    shaped_new = fresh.reshape(row_blocks, NB, col_blocks, NB)
    result = jnp.where(keep_mask[:, None, :, None], shaped_new, shaped_old).reshape(matrix.shape)
    result = result.at[:, :NB].set(jnp.where(col_index == 0, panel, result[:, :NB]))
    return result


def solution(mesh):
    return jax.shard_map(
        body, mesh=mesh, in_specs=(P("row", "col"),), out_specs=P("row", "col"), check_vma=False
    )
```

profile of v0, /device:TPU:0, one launch (start us, length us, event | category | flops | bytes accessed | tf_op | source)
XLA Modules:
  0.0 205.8 jit_solution(1696970586358199093)
XLA Ops:
  6.5 0.8 slice.64
  7.4 0.1 copy.8
  7.5 0.9 bitcast_add_fusion.1
  8.3 0.1 copy.5
  8.5 11.7 %cholesky.19 = f32[128,128]{1,0:T(8,128)S(1)} custom-call(f32[128,128]{1,0:T(8,128)S(1)} %fusion.4), custom_call_target="Cholesky" | custom-call | tf_op jit(solution)/shard_map/jit(cholesky)/cholesky | solution.py:16
  20.2 0.6 compare_reduce_fusion.1
  20.9 0.7 fusion.5
  21.5 9.8 %custom-call.7 = f32[1,128,128]{1,2,0:T(8,128)S(1)} custom-call(f32[1,128,128]{2,1,0:T(8,128)S(1)} %get-tuple-element.30), custom_call_target="InvertDiagBlocksLowerTriangular" | custom-call | tf_op jit(solution)/shard_map/jit(_solve_triangular)/triangular_solve | solution.py:18
  31.3 0.2 convolution_bitcast_fusion.1
  31.6 0.7 maximum_select_fusion
  32.3 57.0 %all-reduce.3.cloned.1.call-done = f32[2,128,128]{2,1,0:T(8,128)} async-done(((f32[2,128,128]{2,1,0:T(8,128)}), f32[2,128,128]{2,1,0:T(8,128)}) %all-reduce.3.cloned.1.call-update) | async-done | bytes 131088 | tf_op jit(solution)/shard_map/psum | solution.py:11
  89.3 1.7 convolution_bitcast_fusion
  91.0 0.9 fusion.2
  91.8 0.8 broadcast_select_fusion
  92.8 44.4 %all-reduce.5.cloned.1.call-done = f32[1024,128]{1,0:T(8,128)} async-done(((f32[1024,128]{1,0:T(8,128)}), f32[1024,128]{1,0:T(8,128)}) %all-reduce.5.cloned.1.call-update) | async-done | bytes 524304 | tf_op jit(solution)/shard_map/psum | solution.py:11
  137.2 0.6 compare_reduce_fusion
  137.9 0.1 broadcast_bitcast_fusion
  138.0 0.1 compare_and_fusion
  138.1 48.0 %all-gather.2.cloned.1.call-done = f32[8192,128]{1,0:T(8,128)} async-done(((f32[1024,128]{1,0:T(8,128)}), f32[8192,128]{1,0:T(8,128)}) %all-gather.2.cloned.1.call-update) | async-done | bytes 4194320 | tf_op jit(solution)/shard_map/all_gather | solution.py:43
  186.1 2.8 %gather_fusion = f32[8,128,128]{2,1,0:T(8,128)S(1)} fusion(f32[64,128,128]{2,1,0:T(8,128)} %bitcast.38, s32[1024]{0:T(1024)S(1)} %pad_clamp_fusion), kind=kCustom, calls=%fused_computation | custom fusion | bytes 1048608 | tf_op jit(solution)/shard_map/jit(_take)/gather | solution.py:47
  188.8 0.2 bitcast_select_fusion
  189.0 0.3 broadcast_in_dim.44
  189.4 7.4 %subtract_select_fusion = f32[1024,1024]{1,0:T(8,128)} fusion(f32[1024,1024]{1,0:T(8,128)} %param.5, pred[128,8,8,128]{3,2,1,0:T(8,128)(4,1)S(1)} %bitcast.37, f32[1024,128]{1,0:T(8,128)} %all-reduce.5.cloned.1.call-done, f32[1024,128]{1,0:T(8,128)S(1)} %bitcast_select_fusion), kind=kOutput, calls=%fused_computation.1 | convolution fusion | flops 1612709888 | bytes 10485760 | tf_op jit(solution)/shard_map/dot_general | solution.py:48
  196.8 2.5 %fusion = f32[1024,1024]{1,0:T(8,128)} fusion(f32[1024,1024]{1,0:T(8,128)} %subtract_select_fusion, f32[1024,128]{1,0:T(8,128)S(1)} %copy-done, pred[]{:T(512)} %compare_reduce_fusion, pred[]{:T(512)S(6)} %eq.6), kind=kLoop, calls=%fused_computation.5 | loop fusion | flops 262144 | bytes 1573377 | tf_op jit(solution)/shard_map/scatter | solution.py:62
  (17 shorter events, 0.2 us)
Async XLA Ops:
  6.5 82.8 %all-reduce.3.cloned.1.call-start = ((), (), s32[]{:S(2)}) async-start(), calls=%async_computation | async-start | bytes 262144 | tf_op jit(solution)/shard_map/psum | solution.py:11
  32.3 104.9 %all-reduce.5.cloned.1.call-start = ((), (), s32[]{:S(2)}) async-start(), calls=%async_computation.1 | async-start | bytes 1048576 | tf_op jit(solution)/shard_map/psum | solution.py:11
  92.7 93.4 %all-gather.2.cloned.1.call-start = ((), (), s32[]{:S(2)}) async-start(), calls=%async_computation.2 | async-start | bytes 4718592 | tf_op jit(solution)/shard_map/all_gather | solution.py:43
  189.4 7.4 %copy-start = (f32[1024,128]{1,0:T(8,128)S(1)}, f32[1024,128]{1,0:T(8,128)}, u32[]{:S(2)}) copy-start(f32[1024,128]{1,0:T(8,128)} %all-reduce.5.cloned.1.call-done) | copy-start | bytes 1572868
Sparse Core Ops, SparseCore 0:
  32.4 56.8 all-reduce.2
  92.8 44.3 all-reduce.4
  138.9 47.1 all-gather.1
where the time goes:
time: 206 us
  waiting for transfers between devices  149 us (72%)
  other arithmetic  29.5 us (14%)
  between operations  13.2 us (6%)
  matrix products  9.34 us (5%)
  local copies, waits for them, and re-layouts  4.2 us (2%)
    psum x2, waiting for transfers between devices, from_root(): return lax.psum(kept, axis)  101 us
    all_gather x1, waiting for transfers between devices, body(): whole = lax.all_gather(panel, 'row', axis=0, tiled=True)  48 us
    another operation x3, other arithmetic, factor(): lower_factor = jnp.linalg.cholesky(symmetric)  12.4 us
    another operation x1, other arithmetic, factor(): jax.scipy.linalg.solve_triangular(lower_factor, identity, lower=True)  9.81 us
    dot_general x1, matrix products, body(): lax.dot_general(panel, mirror, (((1,), (1,)), ((), ())), precision=lax.Pr...  7.43 us
  transfers between devices with their start and end apart: 3, of which 3 were waited for; matrix products, arithmetic and copies ran while one was open for 0% of the time, Pallas kernels for 0%

commit v1 on v0

--- a/solution.py
+++ b/solution.py
@@ -8,7 +8,7 @@
 
 def from_root(value, axis, source):
     kept = jnp.where(lax.axis_index(axis) == source, value, 0).astype(value.dtype)
-    return lax.psum(kept, axis)
+    return jnp.sum(lax.all_gather(kept, axis), axis=0)
 
 
 def factor(corner):

time: 206 us -> 185 us (0.90)
  waiting for transfers between devices: 149 us -> 106 us
  local copies, waits for them, and re-layouts: 4.2 us -> 23.2 us
  other arithmetic: 29.5 us -> 32.4 us
    psum x2 -> x0, waiting for transfers between devices: 101 us -> none  [from_root(): return lax.psum(kept, axis)]
    all_gather x0 -> x2, waiting for transfers between devices: none -> 59.8 us  [from_root(): return jnp.sum(lax.all_gather(kept, axis), axis=0)]
    reshape x0 -> x1, local copies, waits for them, and re-layouts: none -> 5.57 us  [body(): all_blocks = whole.reshape(rows_here * row_blocks, NB, NB)]
    scatter x0 -> x1, local copies, waits for them, and re-layouts: none -> 5.34 us  [body(): result.at[:, :NB].set(jnp.where(col_index == 0, panel, result[:, :NB]))]
    unnamed x3 -> x4, local copies, waits for them, and re-layouts: 0.09 us -> 5.43 us
    reduce_sum x0 -> x2, other arithmetic: none -> 3.54 us  [from_root(): return jnp.sum(lax.all_gather(kept, axis), axis=0)]
    all_gather x0 -> x1, local copies, waits for them, and re-layouts: none -> 2.67 us  [from_root(): return jnp.sum(lax.all_gather(kept, axis), axis=0)]
where the time goes in v1:
time: 185 us; the launch traced here: 184 us
  waiting for transfers between devices  106 us (57%)
  other arithmetic  32.4 us (18%)
  local copies, waits for them, and re-layouts  23.2 us (13%)
  between operations  13.3 us (7%)
  matrix products  8.82 us (5%)
    all_gather x2, waiting for transfers between devices, from_root(): return jnp.sum(lax.all_gather(kept, axis), axis=0)  59.8 us
    all_gather x1, waiting for transfers between devices, body(): whole = lax.all_gather(panel, 'row', axis=0, tiled=True)  46.4 us
    another operation x3, other arithmetic, factor(): lower_factor = jnp.linalg.cholesky(symmetric)  12.5 us
    another operation x1, other arithmetic, factor(): jax.scipy.linalg.solve_triangular(lower_factor, identity, lower=True)  9.81 us
    dot_general x1, matrix products, body(): lax.dot_general(panel, mirror, (((1,), (1,)), ((), ())), precision=lax.Pr...  6.95 us
    reshape x1, local copies, waits for them, and re-layouts, body(): all_blocks = whole.reshape(rows_here * row_blocks, NB, NB)  5.57 us
    unnamed x4, local copies, waits for them, and re-layouts  5.43 us
    scatter x1, local copies, waits for them, and re-layouts, body(): result.at[:, :NB].set(jnp.where(col_index == 0, panel, result[:, :NB]))  5.34 us
  transfers between devices with their start and end apart: 3, of which 3 were waited for; matrix products, arithmetic and copies ran while one was open for 0% of the time, Pallas kernels for 0%

profile of v1, /device:TPU:0, one launch (start us, length us, event | category | flops | bytes accessed | tf_op | source)
XLA Modules:
  0.0 184.2 jit_solution(4354615041114553384)
XLA Ops:
  6.5 5.3 %copy.25 = f32[1024,1024]{0,1:T(8,128)} copy(f32[1024,1024]{1,0:T(8,128)} %param.5) | data formatting | bytes 8388608 | tf_op args[0]
  11.9 0.8 slice.72
  12.8 0.9 bitcast_add_fusion.1
  13.8 11.7 %cholesky.19 = f32[128,128]{1,0:T(8,128)S(1)} custom-call(f32[128,128]{1,0:T(8,128)S(1)} %fusion.4), custom_call_target="Cholesky" | custom-call | tf_op jit(solution)/shard_map/jit(cholesky)/cholesky | solution.py:16
  25.5 0.7 compare_reduce_fusion.1
  26.3 0.7 fusion.5
  27.0 9.8 %custom-call.7 = f32[1,128,128]{1,2,0:T(8,128)S(1)} custom-call(f32[1,128,128]{2,1,0:T(8,128)S(1)} %get-tuple-element.30), custom_call_target="InvertDiagBlocksLowerTriangular" | custom-call | tf_op jit(solution)/shard_map/jit(_solve_triangular)/triangular_solve | solution.py:18
  36.8 0.2 convolution_bitcast_fusion.1
  37.1 0.7 maximum_select_fusion
  37.8 24.9 %all-gather.5.cloned.1.call-done = f32[8,2,128,128]{3,2,1,0:T(8,128)} async-done(((f32[1,2,128,128]{3,2,1,0:T(8,128)}), f32[8,2,128,128]{3,2,1,0:T(8,128)}) %all-gather.5.cloned.1.call-update) | async-done | bytes 1048592 | tf_op jit(solution)/shard_map/all_gather | solution.py:11
  62.7 1.3 reduce_sum.18
  64.0 1.6 convolution_bitcast_fusion
  65.7 0.8 broadcast_select_fusion
  66.8 34.9 %all-gather.9.cloned.1.call-done = f32[4096,128]{0,1:T(8,128)} async-done(((f32[1024,128]{0,1:T(8,128)}), f32[4096,128]{0,1:T(8,128)}) %all-gather.9.cloned.1.call-update) | async-done | bytes 2097168 | tf_op jit(solution)/shard_map/all_gather | solution.py:11
  101.7 2.7 %reshape.255 = f32[4,1024,128]{1,0,2:T(4,128)S(1)} reshape(f32[4096,128]{0,1:T(8,128)} %all-gather.9.cloned.1.call-done) | data formatting | bytes 4194304 | tf_op jit(solution)/shard_map/all_gather | solution.py:11
  104.4 2.3 %reduce_sum.19 = f32[1024,128]{0,1:T(8,128)} reduce(f32[4,1024,128]{1,0,2:T(4,128)S(1)} %reshape.255, f32[]{:T(128)} %constant.153.clone.1), dimensions={0}, to_apply=%region_3.4 | reduce | flops 393216 | bytes 2621444 | tf_op jit(solution)/shard_map/reduce_sum | solution.py:11
  106.7 0.7 compare_reduce_fusion
  107.6 46.4 %all-gather.7.cloned.1.call-done = f32[8192,128]{0,1:T(8,128)} async-done(((f32[1024,128]{0,1:T(8,128)}), f32[8192,128]{0,1:T(8,128)}) %all-gather.7.cloned.1.call-update) | async-done | bytes 4194320 | tf_op jit(solution)/shard_map/all_gather | solution.py:43
  154.0 5.6 %copy.30 = f32[8192,128]{1,0:T(8,128)} copy(f32[8192,128]{0,1:T(8,128)} %all-gather.7.cloned.1.call-done) | data formatting | bytes 8388608 | tf_op jit(solution)/shard_map/reshape | solution.py:44
  159.5 2.8 %gather_fusion = f32[8,128,128]{2,1,0:T(8,128)S(1)} fusion(f32[64,128,128]{2,1,0:T(8,128)} %bitcast.39, s32[1024]{0:T(1024)S(1)} %pad_clamp_fusion), kind=kCustom, calls=%fused_computation | custom fusion | bytes 1048608 | tf_op jit(solution)/shard_map/jit(_take)/gather | solution.py:47
  162.5 0.3 broadcast_in_dim.44
  162.9 6.9 %subtract_select_fusion = f32[1024,1024]{0,1:T(8,128)} fusion(f32[1024,1024]{0,1:T(8,128)} %copy.25, pred[128,8,8,128]{3,2,1,0:T(8,128)(4,1)S(1)} %bitcast.40, f32[1024,128]{0,1:T(8,128)S(1)} %copy-done, f32[1024,128]{1,0:T(8,128)S(1)} %bitcast_select_fusion), kind=kOutput, calls=%fused_computation.1 | convolution fusion | flops 1612709888 | bytes 10485760 | tf_op jit(solution)/shard_map/dot_general | solution.py:48
  169.8 2.5 %fusion = f32[1024,1024]{0,1:T(8,128)} fusion(f32[1024,1024]{0,1:T(8,128)} %subtract_select_fusion, f32[1024,128]{0,1:T(8,128)S(1)} %copy-done, pred[]{:T(512)} %compare_reduce_fusion, pred[]{:T(512)S(6)} %eq.6), kind=kLoop, calls=%fused_computation.5 | loop fusion | flops 262144 | bytes 1573377 | tf_op jit(solution)/shard_map/scatter | solution.py:62
  172.3 5.3 %copy.28 = f32[1024,1024]{1,0:T(8,128)} copy(f32[1024,1024]{0,1:T(8,128)} %fusion) | data formatting | bytes 8388608 | tf_op jit(solution)/shard_map/scatter | solution.py:62
  (25 shorter events, 1.1 us)
Async XLA Ops:
  6.5 56.2 %all-gather.5.cloned.1.call-start = ((), (), s32[]{:S(2)}) async-start(), calls=%async_computation | async-start | bytes 1179648 | tf_op jit(solution)/shard_map/all_gather | solution.py:11
  37.7 64.0 %all-gather.9.cloned.1.call-start = ((), (), s32[]{:S(2)}) async-start(), calls=%async_computation.2 | async-start | bytes 2621440 | tf_op jit(solution)/shard_map/all_gather | solution.py:11
  66.6 87.3 %all-gather.7.cloned.1.call-start = ((), (), s32[]{:S(2)}) async-start(), calls=%async_computation.1 | async-start | bytes 4718592 | tf_op jit(solution)/shard_map/all_gather | solution.py:43
  107.6 55.3 %copy-start = (f32[1024,128]{0,1:T(8,128)S(1)}, f32[1024,128]{0,1:T(8,128)}, u32[]{:S(2)}) copy-start(f32[1024,128]{0,1:T(8,128)} %reduce_sum.19) | copy-start | bytes 1572868
Sparse Core Ops, SparseCore 0:
  37.9 24.7 all-gather.4
  66.7 34.9 all-gather.8
  106.8 47.1 all-gather.6
